TPU v7x, 256 devices: a whole 4x4x8 slice. The times are simulated.
256 devices in a mesh: dp: 2 (over core), ctx: 32 (over z, y), head: 4 (over x).
Axes of the slice: x: 4, y: 4, z: 8, core: 2. Of those that a mesh axis runs over, the one named last changes fastest.
Arguments:
- x_raw: bfloat16 [2, 8192, 8192], P('dp', 'ctx', 'head'), may hold values from -6 to 6
- bc_raw: bfloat16 [2, 8192, 2, 1024], P('dp', 'ctx', None, 'head'), may hold values from -6 to 6
- z_gate: bfloat16 [2, 8192, 8192], P('dp', 'ctx', 'head'), may hold values from -20 to 20
- dt_raw: bfloat16 [2, 128, 8192], P('dp', 'head', 'ctx'), may hold values from -4 to 4
- resets: int32 [2, 8192], P('dp', 'ctx'), may hold values 0 or 1
- conv_x_weight: float32 [4, 8192], P(None, 'head'), may hold values from -3 to 3
- conv_x_bias: float32 [8192], P('head'), may hold values from -1.5 to 1.5
- conv_bc_weight: float32 [4, 2, 1024], P(None, None, 'head'), may hold values from -3 to 3
- conv_bc_bias: float32 [2, 1024], P(None, 'head'), may hold values from -1.5 to 1.5
- a_log: float32 [128], P('head'), may hold values from -9 to 1
- dt_bias: float32 [128], P('head'), may hold values from -13 to -3
- skip_weight: float32 [128], P('head'), may hold values from 0.5 to 2
- norm_gain: float32 [8192], P('head'), may hold values from 0.1 to 1.9
- grad_out: bfloat16 [2, 8192, 8192], P('dp', 'ctx', 'head'), may hold values from -6 to 6
Outputs:
- grad_x: bfloat16 [2, 8192, 8192], P('dp', 'ctx', 'head')
- grad_bc: bfloat16 [2, 8192, 2, 1024], P('dp', 'ctx', None, 'head')
- grad_z: bfloat16 [2, 8192, 8192], P('dp', 'ctx', 'head')
- grad_dt: float32 [2, 128, 8192], P('dp', 'head', 'ctx')
- grad_conv_x_weight: float32 [4, 8192], P(None, 'head')
- grad_conv_x_bias: float32 [8192], P('head')
- grad_conv_bc_weight: float32 [4, 2, 1024], P(None, None, 'head')
- grad_conv_bc_bias: float32 [2, 1024], P(None, 'head')
- grad_a_log: float32 [128], P('head')
- grad_dt_bias: float32 [128], P('head')
- grad_skip: float32 [128], P('head')
- grad_gain: float32 [8192], P('head')
All inputs are finite; a program needn't handle non-finite values. No bound on the sum of `resets` on one device may be relied on, other than what follows from the above.
Results may differ from a plain program's by a relative error of at most 0.01595.
Values may be sent and summed in bfloat16 or wider, within the bound.
A program may use at most 256 MiB of HBM per device.

v0:
```python
import functools
import jax
import jax.numpy as jnp
from jax import lax
from jax.sharding import PartitionSpec as P

HEAD_DIM = 64
NSTATE = 128
CONV = 4
STRETCH = 128
INNER = 8192
norm_eps = 1e-05


def from_behind(value, axis, steps):
    count = lax.axis_size(axis)
    first, last = (max(0, -steps), min(count, count - steps))
    return lax.ppermute(value, axis, [(source, source + steps) for source in range(first, last)])


def entering(value, axis, join, neutral, backward):
    count, mine = (lax.axis_size(axis), lax.axis_index(axis))
    pieces = jax.tree.map(lambda part: lax.all_gather(part, axis), value)
    if backward:
        pieces = jax.tree.map(lambda part: part[::-1], pieces)
        mine = count - 1 - mine
    running = jax.tree.map(
        lambda part, zero: jnp.full_like(part, 0) + jnp.asarray(zero, part.dtype), value, neutral
    )

    def step(position, running):
        longer = join(running, jax.tree.map(lambda part: part[position], pieces))
        return jax.tree.map(lambda new, old: jnp.where(position < mine, new, old), longer, running)

    return lax.fori_loop(0, count - 1, step, running)


def kept(value):
    return lax.optimization_barrier(value)


def causal_conv(extended, counts, weight, conv_bias):
    pad_rows = CONV - 1
    row_count = extended.shape[0] - pad_rows
    shape_tail = (1,) * (extended.ndim - 1)
    summed = conv_bias + weight[0] * extended[pad_rows:]
    for lag_step in range(1, CONV):
        lower = pad_rows - lag_step
        live_mask = (counts[pad_rows:] == counts[lower : lower + row_count]).astype(jnp.float32)
        summed = summed + weight[lag_step] * extended[
            lower : lower + row_count
        ] * live_mask.reshape((row_count,) + shape_tail)
    return kept(jax.nn.silu(summed).astype(jnp.bfloat16))


def rows_to_blocks(array_rows):
    return array_rows.reshape((array_rows.shape[0] // STRETCH, STRETCH) + array_rows.shape[1:])


def steps_to_blocks(steps_dt):
    shape_now = steps_dt.shape
    reshaped = steps_dt.reshape(shape_now[0], shape_now[1], shape_now[2] // STRETCH, STRETCH)
    return jnp.transpose(reshaped, (2, 0, 1, 3))


def from_before(block_c, prior_state, running, resets_seen):
    from_start = jnp.where(resets_seen == 0.0, jnp.exp(running), 0.0)
    state_half = prior_state.astype(jnp.bfloat16)
    carried = jnp.einsum("tgn,ghpn->tghp", block_c, state_half, preferred_element_type=jnp.float32)
    return carried * jnp.transpose(from_start, (2, 0, 1))[..., None]


def keep_factor(running, resets_seen):
    return jnp.where(resets_seen[-1] == 0.0, jnp.exp(running[..., -1]), 0.0)


def block_end(block_x, block_b, block_dt, running, resets_seen):
    to_end = jnp.where(resets_seen == resets_seen[-1], jnp.exp(running[..., -1:] - running), 0.0)
    scaled = (
        block_x.astype(jnp.float32) * jnp.transpose(block_dt * to_end, (2, 0, 1))[..., None]
    ).astype(jnp.bfloat16)
    return jnp.einsum("sghp,sgn->ghpn", scaled, block_b, preferred_element_type=jnp.float32)


def block_terms(prior_state, block_piece, decay_rate):
    block_x, block_b, block_c, block_dt, block_flags = block_piece
    running = jnp.cumsum(-decay_rate[:, :, None] * block_dt, axis=-1)
    resets_seen = jnp.cumsum(block_flags)
    position = jnp.arange(block_flags.shape[0])
    same_doc = (resets_seen[:, None] == resets_seen[None, :]) & (
        position[:, None] >= position[None, :]
    )
    spread = running[..., :, None] - running[..., None, :]
    segment = jnp.where(same_doc, jnp.exp(jnp.where(same_doc, spread, 0.0)), 0.0)
    scores = jnp.einsum("tgn,sgn->gts", block_c, block_b, preferred_element_type=jnp.float32)
    weights = (scores[:, None] * segment * block_dt[:, :, None, :]).astype(jnp.bfloat16)
    within = jnp.einsum("ghts,sghp->tghp", weights, block_x, preferred_element_type=jnp.float32)
    carried = from_before(block_c, prior_state, running, resets_seen)
    fresh_state = block_end(block_x, block_b, block_dt, running, resets_seen)
    next_state = keep_factor(running, resets_seen)[..., None, None] * prior_state + fresh_state
    return (next_state, within + carried)


def scan_blocks(inputs, b_rows, c_rows, steps_dt, decay_rate, reset_flags, state_in):
    row_count = inputs.shape[0]
    pieces = (
        rows_to_blocks(inputs),
        rows_to_blocks(b_rows),
        rows_to_blocks(c_rows),
        steps_to_blocks(steps_dt),
        rows_to_blocks(reset_flags),
    )
    stepper = functools.partial(block_terms, decay_rate=decay_rate)
    final_state, outputs = lax.scan(stepper, state_in, pieces)
    return (outputs.reshape((row_count,) + inputs.shape[1:]), final_state)


def block_ends(inputs, b_rows, steps_dt, decay_rate, reset_flags):

    def block_advance(carried_pair, block_piece):
        product, prior_state = carried_pair
        part_x, part_b, part_dt, part_flags = block_piece
        running = jnp.cumsum(-decay_rate[:, :, None] * part_dt, axis=-1)
        resets_seen = jnp.cumsum(part_flags)
        keep_all = keep_factor(running, resets_seen)
        fresh_state = block_end(part_x, part_b, part_dt, running, resets_seen)
        return ((product * keep_all, keep_all[..., None, None] * prior_state + fresh_state), None)

    start_pair = (
        jnp.ones(decay_rate.shape, jnp.float32),
        jnp.zeros(decay_rate.shape + (HEAD_DIM, NSTATE), jnp.float32),
    )
    pieces = (
        rows_to_blocks(inputs),
        rows_to_blocks(b_rows),
        steps_to_blocks(steps_dt),
        rows_to_blocks(reset_flags),
    )
    end_pair, unused = lax.scan(block_advance, start_pair, pieces)
    return end_pair


def carried_only(c_rows, steps_dt, decay_rate, reset_flags, prior_state):

    def carried_advance(state_now, block_piece):
        part_c, part_dt, part_flags = block_piece
        running = jnp.cumsum(-decay_rate[:, :, None] * part_dt, axis=-1)
        resets_seen = jnp.cumsum(part_flags)
        carried = from_before(part_c, state_now, running, resets_seen)
        return (keep_factor(running, resets_seen)[..., None, None] * state_now, carried)

    pieces = (rows_to_blocks(c_rows), steps_to_blocks(steps_dt), rows_to_blocks(reset_flags))
    final_state, outputs = lax.scan(carried_advance, prior_state, pieces)
    return outputs.reshape((c_rows.shape[0], c_rows.shape[1], steps_dt.shape[1], HEAD_DIM))


def gate_output(y_ssd, inputs, z_in, skip_weight):
    row_count = inputs.shape[0]
    skip_term = skip_weight.reshape(inputs.shape[1], inputs.shape[2])[
        None, :, :, None
    ] * inputs.astype(jnp.float32)
    mixed = kept((y_ssd + skip_term).astype(jnp.bfloat16))
    return mixed.astype(jnp.float32).reshape(row_count, -1) * jax.nn.silu(z_in)


def combine_pairs(earlier, later):
    return (earlier[0] * later[0], later[0][..., None, None] * earlier[1] + later[1])


def per_device(
    x_raw,
    bc_raw,
    z_gate,
    dt_raw,
    resets,
    conv_x_weight,
    conv_x_bias,
    conv_bc_weight,
    conv_bc_bias,
    a_log,
    dt_bias,
    skip_weight,
    norm_gain,
    grad_out,
):
    halo_rows = CONV - 1
    row_count = x_raw.shape[1]
    g_count = bc_raw.shape[3] // NSTATE
    heads_dev = a_log.shape[0]
    per_group = heads_dev // g_count
    reset_flags = resets[0].astype(jnp.float32)
    counts = jnp.cumsum(reset_flags)
    tail_keep = (counts[-halo_rows:] == counts[-1]).astype(jnp.float32)
    tail_half = tail_keep.astype(jnp.bfloat16)
    x_own = x_raw[0]
    bc_own = bc_raw[0]
    x_prev, bc_prev = from_behind(
        (x_own[-halo_rows:] * tail_half[:, None], bc_own[-halo_rows:] * tail_half[:, None, None]),
        "ctx",
        1,
    )
    x_ext = jnp.concatenate([x_prev, x_own]).astype(jnp.float32)
    bc_ext = jnp.concatenate([bc_prev, bc_own]).astype(jnp.float32)
    padded_counts = jnp.concatenate([jnp.zeros((halo_rows,), jnp.float32), counts])
    z_in = z_gate[0].astype(jnp.float32)
    dt_in = dt_raw[0].astype(jnp.float32)

    def conv_part(x_wide, bc_wide, dt_values, cx_weight, cx_bias, cb_weight, cb_bias, bias_dt):
        inputs = causal_conv(x_wide, padded_counts, cx_weight, cx_bias).reshape(
            row_count, g_count, per_group, HEAD_DIM
        )
        bc_conv = causal_conv(bc_wide, padded_counts, cb_weight, cb_bias)
        b_rows = bc_conv[:, 0].reshape(row_count, g_count, NSTATE)
        c_rows = bc_conv[:, 1].reshape(row_count, g_count, NSTATE)
        steps_dt = jax.nn.softplus(dt_values + bias_dt[:, None]).reshape(
            g_count, per_group, row_count
        )
        return (inputs, b_rows, c_rows, steps_dt)

    conv_outs, conv_pull = jax.vjp(
        conv_part,
        x_ext,
        bc_ext,
        dt_in,
        conv_x_weight,
        conv_x_bias,
        conv_bc_weight,
        conv_bc_bias,
        dt_bias,
    )
    inputs, b_rows, c_rows, steps_dt = conv_outs
    decay_rate = jnp.exp(a_log).reshape(g_count, per_group)
    device_decay, device_state = block_ends(inputs, b_rows, steps_dt, decay_rate, reset_flags)
    unit_decay = jnp.ones_like(device_decay)
    prefix_pair = entering(
        (device_decay, device_state),
        "ctx",
        combine_pairs,
        (unit_decay, jnp.zeros_like(device_state)),
        False,
    )
    state_in = prefix_pair[1]

    def ssd_part(block_inputs, block_b, block_c, block_dt, log_rate, prior_state):
        rate_now = jnp.exp(log_rate).reshape(g_count, per_group)
        return scan_blocks(
            block_inputs, block_b, block_c, block_dt, rate_now, reset_flags, prior_state
        )

    ssd_outs, ssd_pull = jax.vjp(ssd_part, inputs, b_rows, c_rows, steps_dt, a_log, state_in)
    y_ssd = ssd_outs[0]
    gated, post_pull = jax.vjp(gate_output, y_ssd, inputs, z_in, skip_weight)
    cotangent = grad_out[0].astype(jnp.float32)
    gained_out = cotangent * norm_gain
    row_totals = lax.psum(
        (jnp.sum(gated * gated, axis=-1), jnp.sum(gated * gained_out, axis=-1)), "head"
    )
    inv_rms = lax.rsqrt(row_totals[0] / INNER + norm_eps)
    d_gated = (
        gained_out * inv_rms[:, None]
        - gated * (inv_rms * inv_rms * inv_rms * row_totals[1] / INNER)[:, None]
    )
    gain_local = jnp.sum(cotangent * gated * inv_rms[:, None], axis=0)
    dy_ssd, d_inputs_post, d_z, d_skip = post_pull(d_gated)
    carried_map = functools.partial(carried_only, c_rows, steps_dt, decay_rate, reset_flags)
    unused_out, carried_pull = jax.vjp(carried_map, state_in)
    direct_adjoint = carried_pull(dy_ssd)[0]
    later_pair = entering(
        (device_decay, direct_adjoint),
        "ctx",
        combine_pairs,
        (unit_decay, jnp.zeros_like(direct_adjoint)),
        True,
    )
    d_inputs, d_b, d_c, d_dt, d_alog, d_state = ssd_pull((dy_ssd, later_pair[1]))
    d_inputs = d_inputs + d_inputs_post
    d_x_ext, d_bc_ext, d_dt_in, d_cxw, d_cxb, d_cbw, d_cbb, d_dt_bias = conv_pull(
        (d_inputs, d_b, d_c, d_dt)
    )
    back_x, back_bc = from_behind((d_x_ext[:halo_rows], d_bc_ext[:halo_rows]), "ctx", -1)
    grad_x_rows = jnp.concatenate(
        [d_x_ext[halo_rows:row_count], d_x_ext[row_count:] + back_x * tail_keep[:, None]]
    )
    grad_bc_rows = jnp.concatenate(
        [d_bc_ext[halo_rows:row_count], d_bc_ext[row_count:] + back_bc * tail_keep[:, None, None]]
    )
    local_terms = (d_cxw, d_cxb, d_cbw, d_cbb, d_alog, d_dt_bias, d_skip, gain_local)
    summed_terms = lax.psum(
        (
            local_terms[0],
            local_terms[1],
            local_terms[2],
            local_terms[3],
            local_terms[4],
            local_terms[5],
            local_terms[6],
            local_terms[7],
        ),
        ("dp", "ctx"),
    )
    grad_scale = float(lax.axis_size("dp") * lax.axis_size("ctx") * row_count) ** (-0.5)
    return (
        grad_x_rows[None].astype(jnp.bfloat16),
        grad_bc_rows[None].astype(jnp.bfloat16),
        d_z[None].astype(jnp.bfloat16),
        d_dt_in[None],
        summed_terms[0] * grad_scale,
        summed_terms[1] * grad_scale,
        summed_terms[2] * grad_scale,
        summed_terms[3] * grad_scale,
        summed_terms[4] * grad_scale,
        summed_terms[5] * grad_scale,
        summed_terms[6] * grad_scale,
        summed_terms[7] * grad_scale,
    )


def solution(mesh):
    return jax.shard_map(
        per_device,
        mesh=mesh,
        in_specs=(
            P("dp", "ctx", "head"),
            P("dp", "ctx", None, "head"),
            P("dp", "ctx", "head"),
            P("dp", "head", "ctx"),
            P("dp", "ctx"),
            P(None, "head"),
            P("head"),
            P(None, None, "head"),
            P(None, "head"),
            P("head"),
            P("head"),
            P("head"),
            P("head"),
            P("dp", "ctx", "head"),
        ),
        out_specs=(
            P("dp", "ctx", "head"),
            P("dp", "ctx", None, "head"),
            P("dp", "ctx", "head"),
            P("dp", "head", "ctx"),
            P(None, "head"),
            P("head"),
            P(None, None, "head"),
            P(None, "head"),
            P("head"),
            P("head"),
            P("head"),
            P("head"),
        ),
        check_vma=False,
    )
```

profile of v0, /device:TPU:128, one launch (start us, length us, event | category | flops | bytes accessed | tf_op | source)
XLA Modules:
  0.0 1191.2 jit_solution(14840181272702812922)
XLA Ops:
  12.5 3.5 collective-permute-start
  17.0 3.5 collective-permute-start.1
  30.2 3.7 multiply_convert_fusion.7
  34.9 3.1 reshape.652
  38.1 3.3 copy.180
  41.4 11.3 while.160
  61.7 10.0 while.158
  74.3 41.9 %all-gather.3 = f32[32,2,16]{2,1,0:T(2,128)S(1)} all-gather(f32[1,2,16]{2,1,0:T(2,128)S(1)} %bitcast.631), channel_id=2, replica_groups=mesh['dp'=2,'ctx'=32,'head'=4] {'ctx'}, dimensions={0}, use_global_device_ids=true | all-gather | bytes 4224 | tf_op jit(solution)/shard_map/all_gather | solution.py:23
  116.3 168.9 %all-gather.7.cloned.1.call-done = f32[64,16,64,128]{3,2,1,0:T(8,128)} async-done(((f32[2,16,64,128]{3,2,1,0:T(8,128)}), f32[64,16,64,128]{3,2,1,0:T(8,128)}) %all-gather.7.cloned.1.call-update) | async-done | bytes 33554448 | tf_op jit(solution)/shard_map/all_gather | solution.py:23
  285.2 46.6 %while.161 = (s32[]{:T(128)}, f32[2,16,64,128]{3,2,1,0:T(8,128)S(1)}, s32[]{:T(128)}, f32[32,2,16]{2,1,0:T(2,128)S(1)}, f32[32,2,16,64,128]{4,3,2,1,0:T(8,128)}, /*index=5*/s32[]{:T(128)}, s32[]{:T(128)}) while((s32[]{:T(128)}, f32[2,16,64,128]{3,2,1,0:T(8,128)S(1)}, s32[]{:T(128)}, f32[32,2,16]{2,1,0:T(2,128)S(1)}, ...), condition=%wide.region_7.8_spmd.clone, body=%wide.region_6.7_spmd.clone.sunk | while | flops 1048580 | bytes 3146225 | solution.py:35
  334.8 110.5 %while.159 = (s32[]{:T(128)}, f32[2,16,64,128]{3,2,1,0:T(8,128)S(1)}, f32[2,128,2,16,64]{1,0,4,3,2:T(2,128)}, pred[2,2,16,128,128]{4,3,2,1,0:T(32,128)(4,1)}, f3...) while((s32[]{:T(128)}, ...), condition=%wide.region_11.12_spmd.clone, body=%wide.region_8.11_spmd.clone.sunk | while | flops 222142656 | bytes 67194320 | solution.py:114
  350.2 25.0 %dynamic_update_slice.324 = f32[2,128,2,16,64]{1,0,4,3,2:T(2,128)} dynamic-update-slice(f32[2,128,2,16,64]{1,0,4,3,2:T(2,128)} %get-tuple-element.3483, f32[1,128,2,16,64]{1,0,4,3,2:T(1,128)} %bitcast.609, s32[]{:T(128)S(6)} %copy.383, s32[]{:T(128)} %constant.352.clone.1..sunk, s32[]{:T(128)} %constant.352.clone.1..sunk, s32[]{:T(128)} %constant.352.clone.1..sunk, s32[]{:T(128)} %constant.352.clone.1..sunk) | dynamic-update-slice | bytes 2097156 | tf_op jit(solution)/shard_map/jvp()/while/body/jit(dynamic_update_index_in_dim)/dynamic_update_slice | solution.py:114
  376.9 4.0 fusion.249
  405.4 25.0 %dynamic_update_slice.324 = f32[2,128,2,16,64]{1,0,4,3,2:T(2,128)} dynamic-update-slice(f32[2,128,2,16,64]{1,0,4,3,2:T(2,128)} %get-tuple-element.3483, f32[1,128,2,16,64]{1,0,4,3,2:T(1,128)} %bitcast.609, s32[]{:T(128)S(6)} %copy.383, s32[]{:T(128)} %constant.352.clone.1..sunk, s32[]{:T(128)} %constant.352.clone.1..sunk, s32[]{:T(128)} %constant.352.clone.1..sunk, s32[]{:T(128)} %constant.352.clone.1..sunk) | dynamic-update-slice | bytes 2097156 | tf_op jit(solution)/shard_map/jvp()/while/body/jit(dynamic_update_index_in_dim)/dynamic_update_slice | solution.py:114
  432.2 4.0 fusion.249
  445.3 4.3 reshape.606
  454.0 10.4 all-reduce.22
  473.8 2.9 copy.210
  479.5 3.1 copy.212
  482.6 4.1 fusion.159
  489.2 210.1 %all-gather.9.cloned.1.call-done = f32[64,16,64,128]{3,2,1,0:T(8,128)} async-done(((f32[2,16,64,128]{3,2,1,0:T(8,128)}), f32[64,16,64,128]{3,2,1,0:T(8,128)}) %all-gather.9.cloned.1.call-update) | async-done | bytes 33554448 | tf_op jit(solution)/shard_map/all_gather | solution.py:23
  699.3 23.3 %rev.7 = f32[32,2,16,64,128]{4,3,2,1,0:T(8,128)} reverse(f32[32,2,16,64,128]{4,3,2,1,0:T(8,128)} %bitcast.608), dimensions={0} | reverse | bytes 67108864 | tf_op jit(solution)/shard_map/rev | solution.py:25
  722.6 46.6 %while.163 = (s32[]{:T(128)}, f32[2,16,64,128]{3,2,1,0:T(8,128)S(1)}, s32[]{:T(128)}, f32[32,2,16]{2,1,0:T(2,128)S(1)}, f32[32,2,16,64,128]{4,3,2,1,0:T(8,128)}, /*index=5*/s32[]{:T(128)}, s32[]{:T(128)}) while((s32[]{:T(128)}, f32[2,16,64,128]{3,2,1,0:T(8,128)S(1)}, s32[]{:T(128)}, f32[32,2,16]{2,1,0:T(2,128)S(1)}, ...), condition=%wide.region_23.24_spmd.clone, body=%wide.region_22.23_spmd.clone.sunk | while | flops 1048580 | bytes 3146225 | solution.py:35
  772.7 91.6 %while.164 = (s32[]{:T(128)}, f32[2,16]{1,0:T(2,128)}, f32[2,16,64,128]{3,2,1,0:T(8,128)S(1)}, bf16[2,128,2,16,64]{1,4,3,2,0:T(8,128)(2,1)}, bf16[2,128,2,128]{3...) while((s32[]{:T(128)}, f32[2,16]{1,0:T(2,128)}, ...), condition=%wide.region_35.36_spmd.clone, body=%wide.region_24.35_spmd.clone.sunk | while | flops 431345728 | bytes 55708368 | solution.py:114
  780.7 5.2 fusion.275
  799.4 3.2 reduce_window_sum.95
  826.5 5.2 fusion.275
  845.2 3.2 reduce_window_sum.95
  867.9 4.3 multiply_reduce_fusion.3
  881.2 5.1 collective-permute-start.2
  887.6 3.1 collective-permute-start.3
  899.3 274.8 %all-reduce.21 = (f32[4,2048]{1,0:T(4,128)S(1)}, f32[2048]{0:T(1024)}, f32[4,2,256]{2,1,0:T(2,128)S(1)}, f32[2,256]{1,0:T(2,128)}, f32[32]{0:T(128)}, /*index=5*/f32[32]{0:T(128)}, f32[32]{0:T(128)}, f32[2048]{0:T(1024)}) all-reduce(f32[4,2048]{1,0:T(4,128)S(1)} %pad_add_fusion.4, ...), channel_id=1, replica_groups=mesh['dp'=2,'ctx'=32,'head'=4] {'dp','ctx'}, use_global_device_ids=true, to_apply=%region_40.41 | all-reduce | flops 14944 | bytes 119552 | tf_op jit(solution)/shard_map/psum | solution.py:288
  (772 shorter events, 321.8 us)
Async XLA Ops:
  7.2 21.0 %copy-start.120 = (f32[2,256]{1,0:T(2,128)S(1)}, f32[2,256]{1,0:T(2,128)}, u32[]{:S(2)}) copy-start(f32[2,256]{1,0:T(2,128)} %param.36) | copy-start | bytes 6148
  7.2 278.0 %all-gather.7.cloned.1.call-start = ((), (), s32[]{:S(2)}) async-start(), calls=%async_computation | async-start | bytes 34603008 | tf_op jit(solution)/shard_map/all_gather | solution.py:23
  12.5 17.1 %collective-permute-start = (bf16[3,2048]{1,0:T(4,128)(2,1)S(1)}, bf16[3,2048]{1,0:T(4,128)(2,1)S(1)}, u32[]{:S(2)}, u32[]{:S(2)}) collective-permute-start(bf16[3,2048]{1,0:T(4,128)(2,1)S(1)} %bitcast_multiply_fusion.16), channel_id=1, source_target_pairs={{0,4},{4,8},{8,12},{12,16},{16,20},{20,24},{24,28},{28,32},{32,36}... | collective-permute-start | bytes 36872 | tf_op jit(solution)/shard_map/ppermute | solution.py:18
  17.0 10.2 collective-permute-start.1
  20.6 8.8 copy-start.86
  20.6 8.8 copy-start.90
  20.6 8.8 copy-start.94
  23.0 6.3 copy-start.48
  53.7 645.6 %all-gather.9.cloned.1.call-start = ((), (), s32[]{:S(2)}) async-start(), calls=%async_computation.1 | async-start | bytes 34603008 | tf_op jit(solution)/shard_map/all_gather | solution.py:23
  376.9 6.4 copy-start.57
  376.9 6.4 copy-start.71
  376.9 6.4 copy-start.75
  376.9 7.3 copy-start.73
  376.9 7.9 copy-start.64
  376.9 7.9 copy-start.66
  394.7 6.3 copy-start.35
  432.2 6.4 copy-start.57
  432.2 6.5 copy-start.71
  432.2 6.5 copy-start.75
  432.2 7.3 copy-start.73
  432.2 7.9 copy-start.64
  432.2 7.9 copy-start.66
  453.1 11.4 copy-start.14
  880.8 10.7 copy-start.49
  880.8 10.7 copy-start.50
  880.8 10.7 copy-start.118
  881.2 12.0 %copy-start.85 = (bf16[1,32,256]{2,1,0:T(8,128)(2,1)S(1)}, bf16[1,32,256]{2,1,0:T(8,128)(2,1)}, u32[]{:S(2)}) copy-start(bf16[1,32,256]{2,1,0:T(8,128)(2,1)} %param.31) | copy-start | bytes 49156
  881.2 300.9 %collective-permute-start.2 = (f32[3,2048]{1,0:T(4,128)S(1)}, f32[3,2048]{1,0:T(4,128)S(1)}, u32[]{:S(2)}, u32[]{:S(2)}) collective-permute-start(f32[3,2048]{1,0:T(4,128)S(1)} %copy-done.101), channel_id=1, source_target_pairs={{4,0},{8,4},{12,8},{16,12},{20,16},{24,20},{28,24},{32,28},{36,32}... | collective-permute-start | bytes 73736 | tf_op jit(solution)/shard_map/ppermute | solution.py:18
  887.6 292.6 %collective-permute-start.3 = (f32[3,2,256]{2,0,1:T(4,128)}, f32[3,2,256]{2,0,1:T(4,128)}, u32[]{:S(2)}, u32[]{:S(2)}) collective-permute-start(f32[3,2,256]{2,0,1:T(4,128)} %pad_add_fusion.5), channel_id=1, source_target_pairs={{4,0},{8,4},{12,8},{16,12},{20,16},{24,20},{28,24},{32,28},{36,32}... | collective-permute-start | bytes 18440 | tf_op jit(solution)/shard_map/ppermute | solution.py:18
  893.2 287.9 %copy-start.55 = (bf16[1,253,2,256]{3,1,2,0:T(8,128)(2,1)S(1)}, bf16[1,253,2,256]{3,1,2,0:T(8,128)(2,1)}, u32[]{:S(2)}) copy-start(bf16[1,253,2,256]{3,1,2,0:T(8,128)(2,1)} %fusion.164) | copy-start | bytes 777220
  1174.0 8.0 copy-start.9
  1174.1 8.0 copy-start.116
  (145 other events, 415.4 us)
Sparse Core Ops, SparseCore 0:
  53.8 231.3 all-gather.6
  471.0 228.2 all-gather.8
where the time goes:
time: 1200 us; the launch traced here: 1190 us
  waiting for transfers between devices  379 us (32%)
  blocking collectives  327 us (27%)
  other arithmetic  217 us (18%)
  local copies, waits for them, and re-layouts  198 us (16%)
  matrix products  32.7 us (3%)
  starting transfers between devices  15.2 us (1%)
  between operations  15 us (1%)
    all_gather x2, waiting for transfers between devices, entering(): pieces = jax.tree.map(lambda part: lax.all_gather(part, axis), value)  379 us
    psum x1, blocking collectives, per_device(): lax.psum((local_terms[0], local_terms[1], local_terms[2], local_terms[3],...  275 us
    select_n x62, other arithmetic, step(): jnp.where(position < mine, new, old)  90.6 us
    dynamic_update_slice x20, local copies, waits for them, and re-layouts, scan_blocks(): final_state, outputs = lax.scan(stepper, state_in, pieces)  65.8 us
    all_gather x1, blocking collectives, entering(): pieces = jax.tree.map(lambda part: lax.all_gather(part, axis), value)  41.9 us
  transfers between devices with their start and end apart: 6, of which 2 were waited for; matrix products, arithmetic and copies ran while one was open for 5% of the time, Pallas kernels for 0%

commit v1 on v0

--- a/solution.py
+++ b/solution.py
@@ -3,6 +3,7 @@
 import jax.numpy as jnp
 from jax import lax
 from jax.sharding import PartitionSpec as P
+from jax.lax import psum
 
 HEAD_DIM = 64
 NSTATE = 128
@@ -10,6 +11,14 @@
 STRETCH = 128
 INNER = 8192
 norm_eps = 1e-05
+
+
+def skins_time(patch, named_axis, ax_name):
+    y_new = psum(psum(patch, named_axis), ax_name)
+    return y_new
+
+
+units_answer = functools.partial(skins_time, named_axis="dp", ax_name="ctx")
 
 
 def from_behind(value, axis, steps):
@@ -285,7 +294,7 @@
         [d_bc_ext[halo_rows:row_count], d_bc_ext[row_count:] + back_bc * tail_keep[:, None, None]]
     )
     local_terms = (d_cxw, d_cxb, d_cbw, d_cbb, d_alog, d_dt_bias, d_skip, gain_local)
-    summed_terms = lax.psum(
+    summed_terms = units_answer(
         (
             local_terms[0],
             local_terms[1],
@@ -295,8 +304,7 @@
             local_terms[5],
             local_terms[6],
             local_terms[7],
-        ),
-        ("dp", "ctx"),
+        )
     )
     grad_scale = float(lax.axis_size("dp") * lax.axis_size("ctx") * row_count) ** (-0.5)
     return (

time: 1200 us -> 1070 us (0.89)
  blocking collectives: 327 us -> 196 us
    psum x1 -> x2, blocking collectives: 275 us -> 143 us  [skins_time(): y_new = psum(psum(patch, named_axis), ax_name)]
  transfers between devices with their start and end apart: 6 -> 6, of which waited for: 2 -> 2; matrix products, arithmetic and copies ran while one was open for 5% -> 6% of each run, Pallas kernels for 0% -> 0%
where the time goes in v1:
time: 1070 us; the launch traced here: 1060 us
  waiting for transfers between devices  379 us (35%)
  other arithmetic  217 us (20%)
  local copies, waits for them, and re-layouts  198 us (19%)
  blocking collectives  196 us (18%)
  matrix products  32.6 us (3%)
  starting transfers between devices  15.2 us (1%)
  between operations  15 us (1%)
    all_gather x2, waiting for transfers between devices, entering(): pieces = jax.tree.map(lambda part: lax.all_gather(part, axis), value)  379 us
    psum x2, blocking collectives, skins_time(): y_new = psum(psum(patch, named_axis), ax_name)  143 us
    select_n x62, other arithmetic, step(): jnp.where(position < mine, new, old)  90.6 us
    dynamic_update_slice x20, local copies, waits for them, and re-layouts, scan_blocks(): final_state, outputs = lax.scan(stepper, state_in, pieces)  66 us
    all_gather x1, blocking collectives, entering(): pieces = jax.tree.map(lambda part: lax.all_gather(part, axis), value)  41.9 us
    rev x2, local copies, waits for them, and re-layouts, entering(): pieces = jax.tree.map(lambda part: part[::-1], pieces)  23.3 us
    dynamic_update_slice x18, other arithmetic, scan_blocks(): final_state, outputs = lax.scan(stepper, state_in, pieces)  22.7 us
  transfers between devices with their start and end apart: 6, of which 2 were waited for; matrix products, arithmetic and copies ran while one was open for 6% of the time, Pallas kernels for 0%

profile of v1, /device:TPU:128, one launch (start us, length us, event | category | flops | bytes accessed | tf_op | source)
XLA Modules:
  0.0 1059.3 jit_solution(10359379535267064781)
XLA Ops:
  12.5 3.5 collective-permute-start
  17.0 3.5 collective-permute-start.1
  30.2 3.8 multiply_convert_fusion.7
  34.9 3.1 reshape.652
  38.0 3.3 copy.180
  41.4 11.3 %while.160 = (s32[]{:T(128)}, f32[2,16]{1,0:T(2,128)S(1)}, f32[2,16,64,128]{3,2,1,0:T(8,128)S(1)}, f32[2,128]{1,0:T(2,128)}, f32[2,16,1]{1,0,2:T(2,128)}, /*inde...) while((s32[]{:T(128)}, f32[2,16]{1,0:T(2,128)S(1)}, ...), condition=%wide.region_5.6_spmd.clone, body=%wide.region_2.5_spmd.clone.sunk | while | flops 69234784 | bytes 2825641 | solution.py:148
  61.6 9.9 while.158
  74.2 41.9 %all-gather.3 = f32[32,2,16]{2,1,0:T(2,128)S(1)} all-gather(f32[1,2,16]{2,1,0:T(2,128)S(1)} %bitcast.631), channel_id=2, replica_groups=mesh['dp'=2,'ctx'=32,'head'=4] {'ctx'}, dimensions={0}, use_global_device_ids=true | all-gather | bytes 4224 | tf_op jit(solution)/shard_map/all_gather | solution.py:32
  116.1 169.0 %all-gather.7.cloned.1.call-done = f32[64,16,64,128]{3,2,1,0:T(8,128)} async-done(((f32[2,16,64,128]{3,2,1,0:T(8,128)}), f32[64,16,64,128]{3,2,1,0:T(8,128)}) %all-gather.7.cloned.1.call-update) | async-done | bytes 33554448 | tf_op jit(solution)/shard_map/all_gather | solution.py:32
  285.1 46.6 %while.161 = (s32[]{:T(128)}, f32[2,16,64,128]{3,2,1,0:T(8,128)S(1)}, s32[]{:T(128)}, f32[32,2,16]{2,1,0:T(2,128)S(1)}, f32[32,2,16,64,128]{4,3,2,1,0:T(8,128)}, /*index=5*/s32[]{:T(128)}, s32[]{:T(128)}) while((s32[]{:T(128)}, f32[2,16,64,128]{3,2,1,0:T(8,128)S(1)}, s32[]{:T(128)}, f32[32,2,16]{2,1,0:T(2,128)S(1)}, ...), condition=%wide.region_7.8_spmd.clone, body=%wide.region_6.7_spmd.clone.sunk | while | flops 1048580 | bytes 3146225 | solution.py:44
  334.8 110.8 %while.159 = (s32[]{:T(128)}, f32[2,16,64,128]{3,2,1,0:T(8,128)S(1)}, f32[2,128,2,16,64]{1,0,4,3,2:T(2,128)}, pred[2,2,16,128,128]{4,3,2,1,0:T(32,128)(4,1)}, f3...) while((s32[]{:T(128)}, ...), condition=%wide.region_11.12_spmd.clone, body=%wide.region_8.11_spmd.clone.sunk | while | flops 222142656 | bytes 67194320 | solution.py:123
  350.2 25.0 %dynamic_update_slice.324 = f32[2,128,2,16,64]{1,0,4,3,2:T(2,128)} dynamic-update-slice(f32[2,128,2,16,64]{1,0,4,3,2:T(2,128)} %get-tuple-element.3491, f32[1,128,2,16,64]{1,0,4,3,2:T(1,128)} %bitcast.609, s32[]{:T(128)S(6)} %copy.383, s32[]{:T(128)} %constant.352.clone.1..sunk, s32[]{:T(128)} %constant.352.clone.1..sunk, s32[]{:T(128)} %constant.352.clone.1..sunk, s32[]{:T(128)} %constant.352.clone.1..sunk) | dynamic-update-slice | bytes 2097156 | tf_op jit(solution)/shard_map/jvp()/while/body/jit(dynamic_update_index_in_dim)/dynamic_update_slice | solution.py:123
  377.0 4.0 fusion.249
  405.6 25.0 %dynamic_update_slice.324 = f32[2,128,2,16,64]{1,0,4,3,2:T(2,128)} dynamic-update-slice(f32[2,128,2,16,64]{1,0,4,3,2:T(2,128)} %get-tuple-element.3491, f32[1,128,2,16,64]{1,0,4,3,2:T(1,128)} %bitcast.609, s32[]{:T(128)S(6)} %copy.383, s32[]{:T(128)} %constant.352.clone.1..sunk, s32[]{:T(128)} %constant.352.clone.1..sunk, s32[]{:T(128)} %constant.352.clone.1..sunk, s32[]{:T(128)} %constant.352.clone.1..sunk) | dynamic-update-slice | bytes 2097156 | tf_op jit(solution)/shard_map/jvp()/while/body/jit(dynamic_update_index_in_dim)/dynamic_update_slice | solution.py:123
  432.4 4.0 fusion.249
  445.6 4.3 reshape.606
  454.4 10.4 all-reduce.22
  479.8 3.1 copy.212
  482.9 4.1 fusion.159
  489.4 210.2 %all-gather.9.cloned.1.call-done = f32[64,16,64,128]{3,2,1,0:T(8,128)} async-done(((f32[2,16,64,128]{3,2,1,0:T(8,128)}), f32[64,16,64,128]{3,2,1,0:T(8,128)}) %all-gather.9.cloned.1.call-update) | async-done | bytes 33554448 | tf_op jit(solution)/shard_map/all_gather | solution.py:32
  699.6 23.3 %rev.7 = f32[32,2,16,64,128]{4,3,2,1,0:T(8,128)} reverse(f32[32,2,16,64,128]{4,3,2,1,0:T(8,128)} %bitcast.608), dimensions={0} | reverse | bytes 67108864 | tf_op jit(solution)/shard_map/rev | solution.py:34
  722.9 46.6 %while.163 = (s32[]{:T(128)}, f32[2,16,64,128]{3,2,1,0:T(8,128)S(1)}, s32[]{:T(128)}, f32[32,2,16]{2,1,0:T(2,128)S(1)}, f32[32,2,16,64,128]{4,3,2,1,0:T(8,128)}, /*index=5*/s32[]{:T(128)}, s32[]{:T(128)}) while((s32[]{:T(128)}, f32[2,16,64,128]{3,2,1,0:T(8,128)S(1)}, s32[]{:T(128)}, f32[32,2,16]{2,1,0:T(2,128)S(1)}, ...), condition=%wide.region_23.24_spmd.clone, body=%wide.region_22.23_spmd.clone.sunk | while | flops 1048580 | bytes 3146225 | solution.py:44
  773.0 91.9 %while.164 = (s32[]{:T(128)}, f32[2,16]{1,0:T(2,128)}, f32[2,16,64,128]{3,2,1,0:T(8,128)S(1)}, bf16[2,128,2,16,64]{1,4,3,2,0:T(8,128)(2,1)}, bf16[2,128,2,128]{3...) while((s32[]{:T(128)}, f32[2,16]{1,0:T(2,128)}, ...), condition=%wide.region_35.36_spmd.clone, body=%wide.region_24.35_spmd.clone.sunk | while | flops 431345728 | bytes 55708368 | solution.py:123
  781.0 5.2 fusion.275
  799.6 3.2 reduce_window_sum.95
  826.9 5.2 fusion.275
  845.6 3.2 reduce_window_sum.95
  868.5 4.3 multiply_reduce_fusion.3
  881.7 5.1 collective-permute-start.2
  888.2 3.1 collective-permute-start.3
  898.8 4.8 all-reduce.23
  903.6 138.6 %all-reduce.21 = (f32[4,2048]{1,0:T(4,128)S(1)}, f32[2048]{0:T(1024)S(1)}, f32[4,2,256]{2,1,0:T(2,128)S(1)}, f32[2,256]{1,0:T(2,128)}, f32[32]{0:T(128)}, /*index=5*/f32[32]{0:T(128)}, f32[32]{0:T(128)}, f32[2048]{0:T(1024)}) all-reduce(f32[4,2048]{1,0:T(4,128)S(1)} %get-tuple-element.2662, ...), channel_id=1, replica_groups=mesh['dp'=2,'ctx'=32,'head'=4] {'ctx'}, use_global_device_ids=true, to_apply=%region_41.42 | all-reduce | flops 14944 | bytes 119552 | tf_op jit(solution)/shard_map/psum | solution.py:17
  (773 shorter events, 324.0 us)
Async XLA Ops:
  7.2 20.9 %copy-start.120 = (f32[2,256]{1,0:T(2,128)S(1)}, f32[2,256]{1,0:T(2,128)}, u32[]{:S(2)}) copy-start(f32[2,256]{1,0:T(2,128)} %param.36) | copy-start | bytes 6148
  7.2 278.0 %all-gather.7.cloned.1.call-start = ((), (), s32[]{:S(2)}) async-start(), calls=%async_computation | async-start | bytes 34603008 | tf_op jit(solution)/shard_map/all_gather | solution.py:32
  12.5 17.1 %collective-permute-start = (bf16[3,2048]{1,0:T(4,128)(2,1)S(1)}, bf16[3,2048]{1,0:T(4,128)(2,1)S(1)}, u32[]{:S(2)}, u32[]{:S(2)}) collective-permute-start(bf16[3,2048]{1,0:T(4,128)(2,1)S(1)} %bitcast_multiply_fusion.16), channel_id=1, source_target_pairs={{0,4},{4,8},{8,12},{12,16},{16,20},{20,24},{24,28},{28,32},{32,36}... | collective-permute-start | bytes 36872 | tf_op jit(solution)/shard_map/ppermute | solution.py:27
  17.0 10.2 collective-permute-start.1
  20.6 8.8 copy-start.86
  20.6 8.8 copy-start.90
  20.6 8.8 copy-start.94
  23.0 6.3 copy-start.48
  53.7 646.0 %all-gather.9.cloned.1.call-start = ((), (), s32[]{:S(2)}) async-start(), calls=%async_computation.1 | async-start | bytes 34603008 | tf_op jit(solution)/shard_map/all_gather | solution.py:32
  339.5 6.3 copy-start.35
  376.9 6.4 copy-start.57
  376.9 6.4 copy-start.71
  376.9 6.4 copy-start.75
  377.0 7.3 copy-start.73
  377.0 7.9 copy-start.64
  377.0 7.9 copy-start.66
  432.3 6.5 copy-start.57
  432.3 6.5 copy-start.71
  432.3 6.5 copy-start.75
  432.3 7.3 copy-start.73
  432.4 7.9 copy-start.64
  432.4 7.9 copy-start.66
  453.4 11.4 %copy-start.14 = (f32[1,256,2048]{1,2,0:T(8,128)S(1)}, f32[1,256,2048]{1,2,0:T(8,128)}, u32[]{:S(2)}) copy-start(f32[1,256,2048]{1,2,0:T(8,128)} %copy.183) | copy-start | bytes 6291460
  881.3 10.7 %copy-start.49 = (f32[2,16,2,128]{1,0,3,2:T(2,128)S(1)}, f32[2,16,2,128]{1,0,3,2:T(2,128)}, u32[]{:S(2)}) copy-start(f32[2,16,2,128]{1,0,3,2:T(2,128)} %copy-done.48) | copy-start | bytes 98308
  881.3 10.7 %copy-start.50 = (f32[2,2,16,128]{2,1,3,0:T(2,128)S(1)}, f32[2,2,16,128]{2,1,3,0:T(2,128)}, u32[]{:S(2)}) copy-start(f32[2,2,16,128]{2,1,3,0:T(2,128)} %get-tuple-element.1723) | copy-start | bytes 98308
  881.3 10.7 %copy-start.118 = (f32[2,16]{1,0:T(2,128)S(1)}, f32[2,16]{1,0:T(2,128)}, u32[]{:S(2)}) copy-start(f32[2,16]{1,0:T(2,128)} %copy-done.117) | copy-start | bytes 388
  881.7 12.0 %copy-start.85 = (bf16[1,32,256]{2,1,0:T(8,128)(2,1)S(1)}, bf16[1,32,256]{2,1,0:T(8,128)(2,1)}, u32[]{:S(2)}) copy-start(bf16[1,32,256]{2,1,0:T(8,128)(2,1)} %param.31) | copy-start | bytes 49156
  881.7 168.4 %collective-permute-start.2 = (f32[3,2048]{1,0:T(4,128)S(1)}, f32[3,2048]{1,0:T(4,128)S(1)}, u32[]{:S(2)}, u32[]{:S(2)}) collective-permute-start(f32[3,2048]{1,0:T(4,128)S(1)} %copy-done.101), channel_id=1, source_target_pairs={{4,0},{8,4},{12,8},{16,12},{20,16},{24,20},{28,24},{32,28},{36,32}... | collective-permute-start | bytes 73736 | tf_op jit(solution)/shard_map/ppermute | solution.py:27
  888.2 160.1 %collective-permute-start.3 = (f32[3,2,256]{2,0,1:T(4,128)}, f32[3,2,256]{2,0,1:T(4,128)}, u32[]{:S(2)}, u32[]{:S(2)}) collective-permute-start(f32[3,2,256]{2,0,1:T(4,128)} %pad_add_fusion.5), channel_id=1, source_target_pairs={{4,0},{8,4},{12,8},{16,12},{20,16},{24,20},{28,24},{32,28},{36,32}... | collective-permute-start | bytes 18440 | tf_op jit(solution)/shard_map/ppermute | solution.py:27
  893.7 155.4 %copy-start.55 = (bf16[1,253,2,256]{3,1,2,0:T(8,128)(2,1)S(1)}, bf16[1,253,2,256]{3,1,2,0:T(8,128)(2,1)}, u32[]{:S(2)}) copy-start(bf16[1,253,2,256]{3,1,2,0:T(8,128)(2,1)} %fusion.164) | copy-start | bytes 777220
  1042.2 8.0 copy-start.9
  1042.2 8.0 copy-start.116
  (145 other events, 416.4 us)
Sparse Core Ops, SparseCore 0:
  53.8 231.3 all-gather.6
  471.3 228.2 all-gather.8
